TPU v7x, 512 devices: a whole 4x4x16 slice. The times are simulated.
512 devices in a mesh: grid: 64 (over y, z_lo, core), band: 8 (over z_hi, x).
Axes of the slice: x: 4, y: 4, z: 16 (z_hi: 2, z_lo: 8; z = z_hi * 8 + z_lo), core: 2. Of those that a mesh axis runs over, the one named last changes fastest.
Arguments:
- orbitals: bfloat16 [32, 64, 16, 32, 128], P('band', 'grid'), may hold values from -7 to 7
- occupations: float32 [32], P('band'), may hold values from 0.5 to 2
- density_in: float32 [64, 16, 32, 128], P('grid'), may hold values from 0.4 to 18
- history_in: bfloat16 [8, 64, 16, 32, 128], P(None, 'grid'), may hold values from 0.29882812 to 3
- history_res: bfloat16 [8, 64, 16, 32, 128], P(None, 'grid'), may hold values from -16 to 16
- screening: float32 [1], replicated, may hold values from 1.5 to 4
Outputs:
- density_next: float32 [64, 16, 32, 128], P('grid')
- residual: float32 [64, 16, 32, 128], P('grid')
All inputs are finite; a program needn't handle non-finite values.
Results may differ from a plain program's by a relative error of at most 0.0003.
Values sent between devices are 32-bit elements; how exact they have to be, the bound alone decides.
A program may use at most 64 MiB of HBM per device.

v0:
```python
import jax
import jax.numpy as jnp
from jax import lax
from jax.sharding import PartitionSpec as P

SWEEPS = 4
mixing_weight = 0.5


def partner(value, axis, apart):
    mask = 2**apart
    pairs = [(source, source ^ mask) for source in range(lax.axis_size(axis))]
    return lax.ppermute(value, axis, pairs)


def shifted(block, axis, distance):
    devices = range(lax.axis_size(axis))
    route = [(i - distance, i) for i in devices if i - distance in devices]
    return lax.ppermute(block, axis, route)


def fetch_whole(field, bit_list):
    for bit in bit_list:
        field = partner(field, "grid", bit)
    return field


def symmetrize(field, fetch, bits_x, bits_y, bits_z):
    field = 0.5 * (field + jnp.flip(fetch(field, bits_x), 1))
    field = 0.5 * (field + jnp.flip(fetch(field, bits_y), 2))
    field = 0.5 * (field + jnp.flip(fetch(field, bits_z), 3))
    return field


def neighbour(face, offset):
    return shifted(face, "grid", offset)


def local(orbitals, occupations, density_in, history_in, history_res, screening):
    n_grid = lax.axis_size("grid")
    grid_bits = n_grid.bit_length() - 1
    waves = orbitals.astype(jnp.float32)
    partial_value = jnp.sum(occupations[:, None, None, None, None] * waves * waves, 0)
    rho_out = lax.psum(partial_value, "band")
    rho_sym = symmetrize(rho_out, fetch_whole, list(range(4, grid_bits)), [2, 3], [0, 1])
    depth = history_res.shape[0]
    res_hist = history_res.astype(jnp.float32)
    charges = lax.psum(jnp.stack([jnp.sum(rho_sym), jnp.sum(density_in)]), "grid")
    scale = charges[1] / charges[0]
    residual = scale * rho_sym - density_in
    vectors = jnp.concatenate([res_hist, residual[None]], 0).reshape(depth + 1, -1)
    local_gram = jnp.dot(vectors, vectors.T, precision=lax.Precision.HIGHEST)
    gram = lax.psum(local_gram, "grid")
    lower = jnp.linalg.cholesky(gram)
    solved = jax.scipy.linalg.cho_solve((lower, True), jnp.ones((depth + 1,), jnp.float32))
    coefficients = solved / jnp.sum(solved)
    rho_opt = (
        jnp.einsum(
            "m,mgxyz->gxyz",
            coefficients[:depth],
            history_in.astype(jnp.float32),
            precision=lax.Precision.HIGHEST,
        )
        + coefficients[depth] * density_in
    )
    res_opt = (
        jnp.einsum("m,mgxyz->gxyz", coefficients[:depth], res_hist, precision=lax.Precision.HIGHEST)
        + coefficients[depth] * residual
    )
    kappa = screening[0]
    index = lax.axis_index("grid")
    block_x = index // 16
    block_y = index // 4 % 4
    block_z = index % 4
    keep_xlow = (block_x > 0).astype(jnp.float32)
    keep_ylow = (block_y > 0).astype(jnp.float32)
    keep_yhigh = (block_y < 3).astype(jnp.float32)
    keep_zlow = (block_z > 0).astype(jnp.float32)
    keep_zhigh = (block_z < 3).astype(jnp.float32)
    source = res_opt[0]
    field_u = jnp.zeros_like(source)
    for sweep in range(SWEEPS):
        x_low = neighbour(field_u[-1:], 16) * keep_xlow
        x_high = neighbour(field_u[:1], -16)
        y_low = neighbour(field_u[:, -1:], 4) * keep_ylow
        y_high = neighbour(field_u[:, :1], -4) * keep_yhigh
        z_low = neighbour(field_u[:, :, -1:], 1) * keep_zlow
        z_high = neighbour(field_u[:, :, :1], -1) * keep_zhigh
        along_x = jnp.concatenate([x_low, field_u, x_high], 0)
        along_y = jnp.concatenate([y_low, field_u, y_high], 1)
        along_z = jnp.concatenate([z_low, field_u, z_high], 2)
        beside = along_x[:-2] + along_x[2:]
        beside = beside + along_y[:, :-2] + along_y[:, 2:]
        beside = beside + along_z[:, :, :-2] + along_z[:, :, 2:]
        field_u = (source + beside) / (6.0 + kappa)
    density_next = rho_opt + mixing_weight * (res_opt - kappa * field_u[None])
    return (density_next, residual)


def solution(mesh):
    in_specs = (
        P("band", "grid", None, None, None),
        P("band"),
        P("grid", None, None, None),
        P(None, "grid", None, None, None),
        P(None, "grid", None, None, None),
        P(),
    )
    out_specs = (P("grid", None, None, None), P("grid", None, None, None))
    return jax.shard_map(local, mesh=mesh, in_specs=in_specs, out_specs=out_specs, check_vma=False)
```

profile of v0, /device:TPU:8, one launch (start us, length us, event | category | flops | bytes accessed | tf_op | source)
XLA Modules:
  0.0 786.0 jit_solution(13246422287680302552)
XLA Ops:
  7.2 2.1 fusion.4
  9.4 158.1 %all-reduce.8.cloned.1.call-done = f32[1,16,32,128]{3,2,1,0:T(8,128)} async-done(((f32[1,16,32,128]{3,2,1,0:T(8,128)}), f32[1,16,32,128]{3,2,1,0:T(8,128)}) %all-reduce.8.cloned.1.call-update) | async-done | bytes 262160 | tf_op jit(solution)/shard_map/psum | solution.py:44
  167.6 2.4 collective-permute-start
  170.0 6.6 collective-permute-done
  176.6 6.1 collective-permute-start.1
  182.8 4.3 collective-permute-done.1
  188.1 2.5 collective-permute-start.2
  190.7 4.4 collective-permute-start.9
  195.1 2.3 collective-permute-start.8
  198.2 2.5 collective-permute-start.11
  204.0 4.8 collective-permute-start.3
  208.8 1.9 copy_convert_fusion
  210.7 27.2 %collective-permute-done.3 = f32[1,16,32,128]{3,2,1,0:T(8,128)S(1)} collective-permute-done((f32[1,16,32,128]{3,2,1,0:T(8,128)S(1)}, f32[1,16,32,128]{3,2,1,0:T(8,128)S(1)}, u32[]{:S(2)}, u32[]{:S(2)}) %collective-permute-start.3) | collective-permute-done | bytes 262176 | tf_op jit(solution)/shard_map/ppermute | solution.py:13
  237.9 3.8 collective-permute-start.6
  244.8 2.0 collective-permute-start.7
  246.8 1.9 collective-permute-start.5
  248.8 8.7 %collective-permute-done.5 = f32[1,16,32,128]{3,2,1,0:T(8,128)} collective-permute-done((f32[1,16,32,128]{3,2,1,0:T(8,128)S(1)}, f32[1,16,32,128]{3,2,1,0:T(8,128)}, u32[]{:S(2)}, u32[]{:S(2)}) %collective-permute-start.5) | collective-permute-done | bytes 262176 | tf_op jit(solution)/shard_map/ppermute | solution.py:13
  261.2 191.7 %psum.22 = f32[2]{0:T(128)S(1)} all-reduce(f32[2]{0:T(128)S(1)} %pad_maximum_fusion.18), channel_id=1, replica_groups=mesh['grid'=64,'band'=8] {'grid'}, use_global_device_ids=true, to_apply=%region_4.5 | all-reduce | flops 2 | bytes 16 | tf_op jit(solution)/shard_map/psum | solution.py:48
  455.9 7.9 %fusion.3 = f32[9,9]{0,1:T(8,128)S(1)} fusion(f32[1,1,16,32,128]{4,0,3,2,1:T(1,128)S(1)} %bitcast.88, f32[8,1,16,32,128]{4,0,3,2,1:T(8,128)} %copy_convert_fusion), kind=kOutput, calls=%fused_computation.5 | convolution fusion | flops 64290816 | bytes 2359620 | tf_op jit(solution)/shard_map/dot_general | solution.py:52
  463.8 193.5 %psum.23 = f32[9,9]{0,1:T(8,128)S(1)} all-reduce(f32[9,9]{0,1:T(8,128)S(1)} %fusion.3), channel_id=1, replica_groups=mesh['grid'=64,'band'=8] {'grid'}, use_global_device_ids=true, to_apply=%region_5.6 | all-reduce | flops 81 | bytes 648 | tf_op jit(solution)/shard_map/psum | solution.py:53
  664.8 1.9 collective-permute-start.16
  666.7 11.1 %collective-permute-start.17 = (f32[16,32,1]{2,1,0:T(8,128)S(1)}, f32[16,32,1]{2,1,0:T(8,128)S(1)}, u32[]{:S(2)}, u32[]{:S(2)}) collective-permute-start(f32[16,32,1]{2,1,0:T(8,128)S(1)} %get-tuple-element.23), channel_id=1, source_target_pairs={{8,0},{16,8},{24,16},{32,24},{40,32},{48,40},{56,48},{64,56},{72,6... | collective-permute-start | bytes 6152 | tf_op jit(solution)/shard_map/ppermute | solution.py:19
  677.9 1.9 collective-permute-start.15
  679.8 4.8 collective-permute-start.14
  684.6 4.4 collective-permute-start.12
  690.4 30.0 %collective-permute-start.13 = (f32[1,32,128]{2,1,0:T(8,128)S(1)}, f32[1,32,128]{2,1,0:T(8,128)S(1)}, u32[]{:S(2)}, u32[]{:S(2)}) collective-permute-start(f32[1,32,128]{2,1,0:T(8,128)S(1)} %get-tuple-element.19), channel_id=1, source_target_pairs={{128,0},{136,8},{144,16},{152,24},{160,32},{168,40},{176,48},{184,... | collective-permute-start | bytes 49160 | tf_op jit(solution)/shard_map/ppermute | solution.py:19
  724.2 11.1 %collective-permute-start.23 = (f32[16,32,1]{2,1,0:T(8,128)S(1)}, f32[16,32,1]{2,1,0:T(8,128)S(1)}, u32[]{:S(2)}, u32[]{:S(2)}) collective-permute-start(f32[16,32,1]{2,1,0:T(8,128)S(1)} %get-tuple-element.17), channel_id=1, source_target_pairs={{8,0},{16,8},{24,16},{32,24},{40,32},{48,40},{56,48},{64,56},{72,6... | collective-permute-start | bytes 6152 | tf_op jit(solution)/shard_map/ppermute | solution.py:19
  737.3 4.8 collective-permute-start.20
  744.0 3.9 collective-permute-start.19
  752.0 11.1 %collective-permute-start.29 = (f32[16,32,1]{2,1,0:T(8,128)S(1)}, f32[16,32,1]{2,1,0:T(8,128)S(1)}, u32[]{:S(2)}, u32[]{:S(2)}) collective-permute-start(f32[16,32,1]{2,1,0:T(8,128)S(1)} %get-tuple-element.11), channel_id=1, source_target_pairs={{8,0},{16,8},{24,16},{32,24},{40,32},{48,40},{56,48},{64,56},{72,6... | collective-permute-start | bytes 6152 | tf_op jit(solution)/shard_map/ppermute | solution.py:19
  765.1 4.8 collective-permute-start.26
  771.9 3.9 collective-permute-start.25
  (102 shorter events, 40.0 us)
Async XLA Ops:
  7.2 681.9 %copy-start = (bf16[8,1,16,32,128]{4,3,2,1,0:T(8,128)(2,1)S(1)}, bf16[8,1,16,32,128]{4,3,2,1,0:T(8,128)(2,1)}, u32[]{:S(2)}) copy-start(bf16[8,1,16,32,128]{4,3,2,1,0:T(8,128)(2,1)} %param.9) | copy-start | bytes 3145732
  7.2 160.4 %all-reduce.8.cloned.1.call-start = ((), (), s32[]{:S(2)}) async-start(), calls=%async_computation | async-start | bytes 524288 | tf_op jit(solution)/shard_map/psum | solution.py:44
  167.6 9.1 %collective-permute-start = (f32[1,16,32,128]{3,2,1,0:T(8,128)}, f32[1,16,32,128]{3,2,1,0:T(8,128)S(1)}, u32[]{:S(2)}, u32[]{:S(2)}) collective-permute-start(f32[1,16,32,128]{3,2,1,0:T(8,128)} %all-reduce.8.cloned.1.call-done), channel_id=1, source_target_pairs={{0,128},{8,136},{16,144},{24,152},{32,160},{40,168},{48,176},{56,1... | collective-permute-start | bytes 786440 | tf_op jit(solution)/shard_map/ppermute | solution.py:13
  176.6 10.5 %collective-permute-start.1 = (f32[1,16,32,128]{3,2,1,0:T(8,128)S(1)}, f32[1,16,32,128]{3,2,1,0:T(8,128)S(1)}, u32[]{:S(2)}, u32[]{:S(2)}) collective-permute-start(f32[1,16,32,128]{3,2,1,0:T(8,128)S(1)} %collective-permute-done), channel_id=1, source_target_pairs={{0,256},{8,264},{16,272},{24,280},{32,288},{40,296},{48,304},{56,3... | collective-permute-start | bytes 786440 | tf_op jit(solution)/shard_map/ppermute | solution.py:13
  188.1 15.9 %collective-permute-start.2 = (f32[1,16,32,128]{3,2,1,0:T(8,128)S(1)}, f32[1,16,32,128]{3,2,1,0:T(8,128)S(1)}, u32[]{:S(2)}, u32[]{:S(2)}) collective-permute-start(f32[1,16,32,128]{3,2,1,0:T(8,128)S(1)} %add_multiply_fusion.1), channel_id=1, source_target_pairs={{0,32},{8,40},{16,48},{24,56},{32,0},{40,8},{48,16},{56,24},{64,96... | collective-permute-start | bytes 786440 | tf_op jit(solution)/shard_map/ppermute | solution.py:13
  190.7 58.1 %collective-permute-start.9 = (f32[16,1,128]{2,1,0:T(1,128)S(1)}, f32[16,1,128]{2,1,0:T(1,128)S(1)}, u32[]{:S(2)}, u32[]{:S(2)}) collective-permute-start(f32[16,1,128]{2,1,0:T(1,128)S(1)} %broadcast.113), channel_id=1, source_target_pairs={{32,0},{40,8},{48,16},{56,24},{64,32},{72,40},{80,48},{88,56},{96,... | collective-permute-start | bytes 24584 | tf_op jit(solution)/shard_map/ppermute | solution.py:19
  195.1 53.7 %collective-permute-start.8 = (f32[16,1,128]{2,1,0:T(1,128)S(1)}, f32[16,1,128]{2,1,0:T(1,128)S(1)}, u32[]{:S(2)}, u32[]{:S(2)}) collective-permute-start(f32[16,1,128]{2,1,0:T(1,128)S(1)} %broadcast.113), channel_id=1, source_target_pairs={{0,32},{8,40},{16,48},{24,56},{32,64},{40,72},{48,80},{56,88},{64,... | collective-permute-start | bytes 24584 | tf_op jit(solution)/shard_map/ppermute | solution.py:19
  198.2 43.7 %collective-permute-start.11 = (f32[16,32,1]{2,1,0:T(8,128)}, f32[16,32,1]{2,1,0:T(8,128)}, u32[]{:S(2)}, u32[]{:S(2)}) collective-permute-start(f32[16,32,1]{2,1,0:T(8,128)} %broadcast.114), channel_id=1, source_target_pairs={{8,0},{16,8},{24,16},{32,24},{40,32},{48,40},{56,48},{64,56},{72,6... | collective-permute-start | bytes 6152 | tf_op jit(solution)/shard_map/ppermute | solution.py:19
  200.7 44.1 %collective-permute-start.10 = (f32[16,32,1]{2,1,0:T(8,128)}, f32[16,32,1]{2,1,0:T(8,128)S(1)}, u32[]{:S(2)}, u32[]{:S(2)}) collective-permute-start(f32[16,32,1]{2,1,0:T(8,128)} %broadcast.114), channel_id=1, source_target_pairs={{0,8},{8,16},{16,24},{24,32},{32,40},{40,48},{48,56},{56,64},{64,7... | collective-permute-start | bytes 6152 | tf_op jit(solution)/shard_map/ppermute | solution.py:19
  204.0 33.9 %collective-permute-start.3 = (f32[1,16,32,128]{3,2,1,0:T(8,128)S(1)}, f32[1,16,32,128]{3,2,1,0:T(8,128)S(1)}, u32[]{:S(2)}, u32[]{:S(2)}) collective-permute-start(f32[1,16,32,128]{3,2,1,0:T(8,128)S(1)} %collective-permute-done.2), channel_id=1, source_target_pairs={{0,64},{8,72},{16,80},{24,88},{32,96},{40,104},{48,112},{56,120},{... | collective-permute-start | bytes 786440 | tf_op jit(solution)/shard_map/ppermute | solution.py:13
  237.9 23.3 %collective-permute-start.6 = (f32[1,32,128]{2,1,0:T(8,128)S(1)}, f32[1,32,128]{2,1,0:T(8,128)S(1)}, u32[]{:S(2)}, u32[]{:S(2)}) collective-permute-start(f32[1,32,128]{2,1,0:T(8,128)S(1)} %broadcast.112), channel_id=1, source_target_pairs={{0,128},{8,136},{16,144},{24,152},{32,160},{40,168},{48,176},{56,1... | collective-permute-start | bytes 49160 | tf_op jit(solution)/shard_map/ppermute | solution.py:19
  241.9 4.9 collective-permute-start.4
  244.8 419.0 %collective-permute-start.7 = (f32[1,32,128]{2,1,0:T(8,128)S(1)}, f32[1,32,128]{2,1,0:T(8,128)S(1)}, u32[]{:S(2)}, u32[]{:S(2)}) collective-permute-start(f32[1,32,128]{2,1,0:T(8,128)S(1)} %broadcast.112), channel_id=1, source_target_pairs={{128,0},{136,8},{144,16},{152,24},{160,32},{168,40},{176,48},{184,... | collective-permute-start | bytes 49160 | tf_op jit(solution)/shard_map/ppermute | solution.py:19
  246.8 10.7 %collective-permute-start.5 = (f32[1,16,32,128]{3,2,1,0:T(8,128)S(1)}, f32[1,16,32,128]{3,2,1,0:T(8,128)}, u32[]{:S(2)}, u32[]{:S(2)}) collective-permute-start(f32[1,16,32,128]{3,2,1,0:T(8,128)S(1)} %collective-permute-done.4), channel_id=1, source_target_pairs={{0,16},{8,24},{16,0},{24,8},{32,48},{40,56},{48,32},{56,40},{64,80... | collective-permute-start | bytes 786440 | tf_op jit(solution)/shard_map/ppermute | solution.py:13
  664.8 25.6 %collective-permute-start.16 = (f32[16,32,1]{2,1,0:T(8,128)S(1)}, f32[16,32,1]{2,1,0:T(8,128)S(1)}, u32[]{:S(2)}, u32[]{:S(2)}) collective-permute-start(f32[16,32,1]{2,1,0:T(8,128)S(1)} %get-tuple-element.22), channel_id=1, source_target_pairs={{0,8},{8,16},{16,24},{24,32},{32,40},{40,48},{48,56},{56,64},{64,7... | collective-permute-start | bytes 6152 | tf_op jit(solution)/shard_map/ppermute | solution.py:19
  666.7 53.7 %collective-permute-start.17 = (f32[16,32,1]{2,1,0:T(8,128)S(1)}, f32[16,32,1]{2,1,0:T(8,128)S(1)}, u32[]{:S(2)}, u32[]{:S(2)}) collective-permute-start(f32[16,32,1]{2,1,0:T(8,128)S(1)} %get-tuple-element.23), channel_id=1, source_target_pairs={{8,0},{16,8},{24,16},{32,24},{40,32},{48,40},{56,48},{64,56},{72,6... | collective-permute-start | bytes 6152 | tf_op jit(solution)/shard_map/ppermute | solution.py:19
  677.9 42.6 %collective-permute-start.15 = (f32[16,1,128]{2,1,0:T(1,128)S(1)}, f32[16,1,128]{2,1,0:T(1,128)S(1)}, u32[]{:S(2)}, u32[]{:S(2)}) collective-permute-start(f32[16,1,128]{2,1,0:T(1,128)S(1)} %get-tuple-element.21), channel_id=1, source_target_pairs={{32,0},{40,8},{48,16},{56,24},{64,32},{72,40},{80,48},{88,56},{96,... | collective-permute-start | bytes 24584 | tf_op jit(solution)/shard_map/ppermute | solution.py:19
  679.8 40.7 %collective-permute-start.14 = (f32[16,1,128]{2,1,0:T(1,128)S(1)}, f32[16,1,128]{2,1,0:T(1,128)S(1)}, u32[]{:S(2)}, u32[]{:S(2)}) collective-permute-start(f32[16,1,128]{2,1,0:T(1,128)S(1)} %get-tuple-element.20), channel_id=1, source_target_pairs={{0,32},{8,40},{16,48},{24,56},{32,64},{40,72},{48,80},{56,88},{64,... | collective-permute-start | bytes 24584 | tf_op jit(solution)/shard_map/ppermute | solution.py:19
  684.6 35.9 %collective-permute-start.12 = (f32[1,32,128]{2,1,0:T(8,128)S(1)}, f32[1,32,128]{2,1,0:T(8,128)S(1)}, u32[]{:S(2)}, u32[]{:S(2)}) collective-permute-start(f32[1,32,128]{2,1,0:T(8,128)S(1)} %get-tuple-element.18), channel_id=1, source_target_pairs={{0,128},{8,136},{16,144},{24,152},{32,160},{40,168},{48,176},{56,1... | collective-permute-start | bytes 49160 | tf_op jit(solution)/shard_map/ppermute | solution.py:19
  690.4 31.4 %collective-permute-start.13 = (f32[1,32,128]{2,1,0:T(8,128)S(1)}, f32[1,32,128]{2,1,0:T(8,128)S(1)}, u32[]{:S(2)}, u32[]{:S(2)}) collective-permute-start(f32[1,32,128]{2,1,0:T(8,128)S(1)} %get-tuple-element.19), channel_id=1, source_target_pairs={{128,0},{136,8},{144,16},{152,24},{160,32},{168,40},{176,48},{184,... | collective-permute-start | bytes 49160 | tf_op jit(solution)/shard_map/ppermute | solution.py:19
  722.2 21.8 %collective-permute-start.22 = (f32[16,32,1]{2,1,0:T(8,128)S(1)}, f32[16,32,1]{2,1,0:T(8,128)S(1)}, u32[]{:S(2)}, u32[]{:S(2)}) collective-permute-start(f32[16,32,1]{2,1,0:T(8,128)S(1)} %get-tuple-element.16), channel_id=1, source_target_pairs={{0,8},{8,16},{16,24},{24,32},{32,40},{40,48},{48,56},{56,64},{64,7... | collective-permute-start | bytes 6152 | tf_op jit(solution)/shard_map/ppermute | solution.py:19
  724.2 23.8 %collective-permute-start.23 = (f32[16,32,1]{2,1,0:T(8,128)S(1)}, f32[16,32,1]{2,1,0:T(8,128)S(1)}, u32[]{:S(2)}, u32[]{:S(2)}) collective-permute-start(f32[16,32,1]{2,1,0:T(8,128)S(1)} %get-tuple-element.17), channel_id=1, source_target_pairs={{8,0},{16,8},{24,16},{32,24},{40,32},{48,40},{56,48},{64,56},{72,6... | collective-permute-start | bytes 6152 | tf_op jit(solution)/shard_map/ppermute | solution.py:19
  735.3 12.7 %collective-permute-start.21 = (f32[16,1,128]{2,1,0:T(1,128)S(1)}, f32[16,1,128]{2,1,0:T(1,128)S(1)}, u32[]{:S(2)}, u32[]{:S(2)}) collective-permute-start(f32[16,1,128]{2,1,0:T(1,128)S(1)} %get-tuple-element.15), channel_id=1, source_target_pairs={{32,0},{40,8},{48,16},{56,24},{64,32},{72,40},{80,48},{88,56},{96,... | collective-permute-start | bytes 24584 | tf_op jit(solution)/shard_map/ppermute | solution.py:19
  737.3 12.1 %collective-permute-start.20 = (f32[16,1,128]{2,1,0:T(1,128)S(1)}, f32[16,1,128]{2,1,0:T(1,128)S(1)}, u32[]{:S(2)}, u32[]{:S(2)}) collective-permute-start(f32[16,1,128]{2,1,0:T(1,128)S(1)} %get-tuple-element.14), channel_id=1, source_target_pairs={{0,32},{8,40},{16,48},{24,56},{32,64},{40,72},{48,80},{56,88},{64,... | collective-permute-start | bytes 24584 | tf_op jit(solution)/shard_map/ppermute | solution.py:19
  742.1 7.3 collective-permute-start.18
  744.0 5.6 collective-permute-start.19
  750.1 21.8 %collective-permute-start.28 = (f32[16,32,1]{2,1,0:T(8,128)S(1)}, f32[16,32,1]{2,1,0:T(8,128)S(1)}, u32[]{:S(2)}, u32[]{:S(2)}) collective-permute-start(f32[16,32,1]{2,1,0:T(8,128)S(1)} %get-tuple-element.10), channel_id=1, source_target_pairs={{0,8},{8,16},{16,24},{24,32},{32,40},{40,48},{48,56},{56,64},{64,7... | collective-permute-start | bytes 6152 | tf_op jit(solution)/shard_map/ppermute | solution.py:19
  752.0 23.8 %collective-permute-start.29 = (f32[16,32,1]{2,1,0:T(8,128)S(1)}, f32[16,32,1]{2,1,0:T(8,128)S(1)}, u32[]{:S(2)}, u32[]{:S(2)}) collective-permute-start(f32[16,32,1]{2,1,0:T(8,128)S(1)} %get-tuple-element.11), channel_id=1, source_target_pairs={{8,0},{16,8},{24,16},{32,24},{40,32},{48,40},{56,48},{64,56},{72,6... | collective-permute-start | bytes 6152 | tf_op jit(solution)/shard_map/ppermute | solution.py:19
  763.2 12.7 %collective-permute-start.27 = (f32[16,1,128]{2,1,0:T(1,128)S(1)}, f32[16,1,128]{2,1,0:T(1,128)S(1)}, u32[]{:S(2)}, u32[]{:S(2)}) collective-permute-start(f32[16,1,128]{2,1,0:T(1,128)S(1)} %get-tuple-element.9), channel_id=1, source_target_pairs={{32,0},{40,8},{48,16},{56,24},{64,32},{72,40},{80,48},{88,56},{96,... | collective-permute-start | bytes 24584 | tf_op jit(solution)/shard_map/ppermute | solution.py:19
  765.1 12.1 %collective-permute-start.26 = (f32[16,1,128]{2,1,0:T(1,128)S(1)}, f32[16,1,128]{2,1,0:T(1,128)S(1)}, u32[]{:S(2)}, u32[]{:S(2)}) collective-permute-start(f32[16,1,128]{2,1,0:T(1,128)S(1)} %get-tuple-element.8), channel_id=1, source_target_pairs={{0,32},{8,40},{16,48},{24,56},{32,64},{40,72},{48,80},{56,88},{64,... | collective-permute-start | bytes 24584 | tf_op jit(solution)/shard_map/ppermute | solution.py:19
  770.0 7.3 collective-permute-start.24
  771.9 5.6 collective-permute-start.25
  (3 other events, 605.0 us)
Sparse Core Ops, SparseCore 0:
  11.5 155.9 all-reduce.7
where the time goes:
time: 787 us; the launch traced here: 786 us
  blocking collectives  385 us (49%)
  waiting for transfers between devices  210 us (27%)
  starting transfers between devices  142 us (18%)
  other arithmetic  17 us (2%)
  between operations  16.8 us (2%)
  matrix products  11.4 us (1%)
    psum x1, blocking collectives, local(): gram = lax.psum(local_gram, 'grid')  194 us
    psum x1, blocking collectives, local(): lax.psum(jnp.stack([jnp.sum(rho_sym), jnp.sum(density_in)]), 'grid')  192 us
    psum x1, waiting for transfers between devices, local(): rho_out = lax.psum(partial_value, 'band')  158 us
    ppermute x24, starting transfers between devices, shifted(): return lax.ppermute(block, axis, route)  123 us
    ppermute x6, waiting for transfers between devices, partner(): return lax.ppermute(value, axis, pairs)  46.9 us
    ppermute x6, starting transfers between devices, partner(): return lax.ppermute(value, axis, pairs)  19.7 us
  transfers between devices with their start and end apart: 31, of which 10 were waited for; matrix products, arithmetic and copies ran while one was open for 3% of the time, Pallas kernels for 0%

commit v1 on v0

--- a/solution.py
+++ b/solution.py
@@ -41,7 +41,13 @@
     grid_bits = n_grid.bit_length() - 1
     waves = orbitals.astype(jnp.float32)
     partial_value = jnp.sum(occupations[:, None, None, None, None] * waves * waves, 0)
-    rho_out = lax.psum(partial_value, "band")
+
+    def seats_all_drive(block_in):
+        a_now = lax.all_gather(block_in, axis_name="band")
+        reply = jnp.sum(a_now, axis=0)
+        return reply
+
+    rho_out = seats_all_drive(partial_value)
     rho_sym = symmetrize(rho_out, fetch_whole, list(range(4, grid_bits)), [2, 3], [0, 1])
     depth = history_res.shape[0]
     res_hist = history_res.astype(jnp.float32)

time: 787 us -> 756 us (0.961)
  the two profiles are of different devices: /device:TPU:8 before, /device:TPU:2 now
where the time goes in v1:
time: 756 us; the launch traced here: 754 us
  blocking collectives  426 us (56%)
  waiting for transfers between devices  185 us (24%)
  starting transfers between devices  93.3 us (12%)
  other arithmetic  17.8 us (2%)
  between operations  16.8 us (2%)
  matrix products  11.4 us (2%)
    psum x1, blocking collectives, local(): lax.psum(jnp.stack([jnp.sum(rho_sym), jnp.sum(density_in)]), 'grid')  213 us
    psum x1, blocking collectives, local(): gram = lax.psum(local_gram, 'grid')  213 us
    all_gather x1, waiting for transfers between devices, seats_all_drive(): a_now = lax.all_gather(block_in, axis_name='band')  124 us
    ppermute x24, starting transfers between devices, shifted(): return lax.ppermute(block, axis, route)  76.3 us
    ppermute x6, waiting for transfers between devices, partner(): return lax.ppermute(value, axis, pairs)  49 us
    ppermute x6, starting transfers between devices, partner(): return lax.ppermute(value, axis, pairs)  16.9 us
  transfers between devices with their start and end apart: 31, of which 8 were waited for; matrix products, arithmetic and copies ran while one was open for 3% of the time, Pallas kernels for 0%

profile of v1, /device:TPU:2, one launch (start us, length us, event | category | flops | bytes accessed | tf_op | source)
XLA Modules:
  0.0 754.4 jit_solution(35098139547245458)
XLA Ops:
  7.2 2.1 fusion.4
  9.4 123.7 %all-gather.3.cloned.1.call-done = f32[128,32,128]{2,1,0:T(8,128)} async-done(((f32[16,32,128]{2,1,0:T(8,128)}), f32[128,32,128]{2,1,0:T(8,128)}) %all-gather.3.cloned.1.call-update) | async-done | bytes 2097168 | tf_op jit(solution)/shard_map/all_gather | solution.py:46
  133.1 1.8 reduce.8
  134.9 2.7 collective-permute-start
  137.6 6.9 collective-permute-done
  144.5 3.0 collective-permute-start.1
  147.5 7.2 collective-permute-done.1
  154.7 2.3 collective-permute-start.2
  158.3 5.4 collective-permute-start.8
  165.8 3.0 collective-permute-start.10
  170.2 5.1 collective-permute-start.3
  175.3 1.9 copy_convert_fusion
  177.2 26.2 %collective-permute-done.3 = f32[1,16,32,128]{3,2,1,0:T(8,128)S(1)} collective-permute-done((f32[1,16,32,128]{3,2,1,0:T(8,128)S(1)}, f32[1,16,32,128]{3,2,1,0:T(8,128)S(1)}, u32[]{:S(2)}, u32[]{:S(2)}) %collective-permute-start.3) | collective-permute-done | bytes 262176 | tf_op jit(solution)/shard_map/ppermute | solution.py:13
  203.5 5.9 collective-permute-start.6
  209.6 1.9 collective-permute-start.4
  213.8 1.9 collective-permute-start.5
  215.8 8.7 %collective-permute-done.5 = f32[1,16,32,128]{3,2,1,0:T(8,128)} collective-permute-done((f32[1,16,32,128]{3,2,1,0:T(8,128)S(1)}, f32[1,16,32,128]{3,2,1,0:T(8,128)}, u32[]{:S(2)}, u32[]{:S(2)}) %collective-permute-start.5) | collective-permute-done | bytes 262176 | tf_op jit(solution)/shard_map/ppermute | solution.py:13
  225.6 1.3 multiply_reduce_fusion
  228.2 213.2 %psum.14 = f32[2]{0:T(128)S(1)} all-reduce(f32[2]{0:T(128)S(1)} %pad_maximum_fusion.18), channel_id=1, replica_groups=mesh['grid'=64,'band'=8] {'grid'}, use_global_device_ids=true, to_apply=%region_4.5 | all-reduce | flops 2 | bytes 16 | tf_op jit(solution)/shard_map/psum | solution.py:54
  444.4 8.0 %fusion.3 = f32[9,9]{0,1:T(8,128)S(1)} fusion(f32[1,1,16,32,128]{4,0,3,2,1:T(1,128)S(1)} %bitcast.91, f32[8,1,16,32,128]{4,0,3,2,1:T(8,128)} %copy_convert_fusion), kind=kOutput, calls=%fused_computation.5 | convolution fusion | flops 64290816 | bytes 2359620 | tf_op jit(solution)/shard_map/dot_general | solution.py:58
  452.3 212.8 %psum.15 = f32[9,9]{0,1:T(8,128)S(1)} all-reduce(f32[9,9]{0,1:T(8,128)S(1)} %fusion.3), channel_id=1, replica_groups=mesh['grid'=64,'band'=8] {'grid'}, use_global_device_ids=true, to_apply=%region_5.6 | all-reduce | flops 81 | bytes 648 | tf_op jit(solution)/shard_map/psum | solution.py:59
  672.5 1.6 collective-permute-start.16
  676.8 5.4 collective-permute-start.14
  686.2 4.2 collective-permute-done.13
  690.9 1.3 collective-permute-start.22
  694.8 5.5 collective-permute-start.20
  700.4 12.0 %collective-permute-start.18 = (f32[1,32,128]{2,1,0:T(8,128)S(1)}, f32[1,32,128]{2,1,0:T(8,128)S(1)}, u32[]{:S(2)}, u32[]{:S(2)}) collective-permute-start(f32[1,32,128]{2,1,0:T(8,128)S(1)} %get-tuple-element.12), channel_id=1, source_target_pairs={{0,128},{8,136},{16,144},{24,152},{32,160},{40,168},{48,176},{56,1... | collective-permute-start | bytes 49160 | tf_op jit(solution)/shard_map/ppermute | solution.py:19
  713.8 4.2 collective-permute-done.19
  722.4 5.5 collective-permute-start.26
  727.9 12.3 %collective-permute-start.24 = (f32[1,32,128]{2,1,0:T(8,128)S(1)}, f32[1,32,128]{2,1,0:T(8,128)S(1)}, u32[]{:S(2)}, u32[]{:S(2)}) collective-permute-start(f32[1,32,128]{2,1,0:T(8,128)S(1)} %get-tuple-element.6), channel_id=1, source_target_pairs={{0,128},{8,136},{16,144},{24,152},{32,160},{40,168},{48,176},{56,1... | collective-permute-start | bytes 49160 | tf_op jit(solution)/shard_map/ppermute | solution.py:19
  741.7 4.2 collective-permute-done.25
  745.9 1.6 fusion.23
  (103 shorter events, 34.4 us)
Async XLA Ops:
  7.2 676.4 %copy-start = (bf16[8,1,16,32,128]{4,3,2,1,0:T(8,128)(2,1)S(1)}, bf16[8,1,16,32,128]{4,3,2,1,0:T(8,128)(2,1)}, u32[]{:S(2)}) copy-start(bf16[8,1,16,32,128]{4,3,2,1,0:T(8,128)(2,1)} %param.9) | copy-start | bytes 3145732
  7.2 125.9 %all-gather.3.cloned.1.call-start = ((), (), s32[]{:S(2)}) async-start(), calls=%async_computation | async-start | bytes 2359296 | tf_op jit(solution)/shard_map/all_gather | solution.py:46
  134.9 9.6 %collective-permute-start = (f32[1,16,32,128]{3,2,1,0:T(8,128)S(1)}, f32[1,16,32,128]{3,2,1,0:T(8,128)S(1)}, u32[]{:S(2)}, u32[]{:S(2)}) collective-permute-start(f32[1,16,32,128]{3,2,1,0:T(8,128)S(1)} %bitcast.88), channel_id=1, source_target_pairs={{0,128},{8,136},{16,144},{24,152},{32,160},{40,168},{48,176},{56,1... | collective-permute-start | bytes 786440 | tf_op jit(solution)/shard_map/ppermute | solution.py:13
  144.5 10.1 %collective-permute-start.1 = (f32[1,16,32,128]{3,2,1,0:T(8,128)S(1)}, f32[1,16,32,128]{3,2,1,0:T(8,128)S(1)}, u32[]{:S(2)}, u32[]{:S(2)}) collective-permute-start(f32[1,16,32,128]{3,2,1,0:T(8,128)S(1)} %collective-permute-done), channel_id=1, source_target_pairs={{0,256},{8,264},{16,272},{24,280},{32,288},{40,296},{48,304},{56,3... | collective-permute-start | bytes 786440 | tf_op jit(solution)/shard_map/ppermute | solution.py:13
  154.7 15.6 %collective-permute-start.2 = (f32[1,16,32,128]{3,2,1,0:T(8,128)S(1)}, f32[1,16,32,128]{3,2,1,0:T(8,128)S(1)}, u32[]{:S(2)}, u32[]{:S(2)}) collective-permute-start(f32[1,16,32,128]{3,2,1,0:T(8,128)S(1)} %add_multiply_fusion.1), channel_id=1, source_target_pairs={{0,32},{8,40},{16,48},{24,56},{32,0},{40,8},{48,16},{56,24},{64,96... | collective-permute-start | bytes 786440 | tf_op jit(solution)/shard_map/ppermute | solution.py:13
  157.0 58.7 %collective-permute-start.9 = (f32[16,1,128]{2,1,0:T(1,128)S(1)}, f32[16,1,128]{2,1,0:T(1,128)S(1)}, u32[]{:S(2)}, u32[]{:S(2)}) collective-permute-start(f32[16,1,128]{2,1,0:T(1,128)S(1)} %broadcast.113), channel_id=1, source_target_pairs={{32,0},{40,8},{48,16},{56,24},{64,32},{72,40},{80,48},{88,56},{96,... | collective-permute-start | bytes 24584 | tf_op jit(solution)/shard_map/ppermute | solution.py:19
  158.3 57.5 %collective-permute-start.8 = (f32[16,1,128]{2,1,0:T(1,128)S(1)}, f32[16,1,128]{2,1,0:T(1,128)S(1)}, u32[]{:S(2)}, u32[]{:S(2)}) collective-permute-start(f32[16,1,128]{2,1,0:T(1,128)S(1)} %broadcast.113), channel_id=1, source_target_pairs={{0,32},{8,40},{16,48},{24,56},{32,64},{40,72},{48,80},{56,88},{64,... | collective-permute-start | bytes 24584 | tf_op jit(solution)/shard_map/ppermute | solution.py:19
  164.5 45.1 %collective-permute-start.11 = (f32[16,32,1]{2,1,0:T(8,128)}, f32[16,32,1]{2,1,0:T(8,128)}, u32[]{:S(2)}, u32[]{:S(2)}) collective-permute-start(f32[16,32,1]{2,1,0:T(8,128)} %broadcast.114), channel_id=1, source_target_pairs={{8,0},{16,8},{24,16},{32,24},{40,32},{48,40},{56,48},{64,56},{72,6... | collective-permute-start | bytes 6152 | tf_op jit(solution)/shard_map/ppermute | solution.py:19
  165.8 46.7 %collective-permute-start.10 = (f32[16,32,1]{2,1,0:T(8,128)}, f32[16,32,1]{2,1,0:T(8,128)S(1)}, u32[]{:S(2)}, u32[]{:S(2)}) collective-permute-start(f32[16,32,1]{2,1,0:T(8,128)} %broadcast.114), channel_id=1, source_target_pairs={{0,8},{8,16},{16,24},{24,32},{32,40},{40,48},{48,56},{56,64},{64,7... | collective-permute-start | bytes 6152 | tf_op jit(solution)/shard_map/ppermute | solution.py:19
  170.2 33.3 %collective-permute-start.3 = (f32[1,16,32,128]{3,2,1,0:T(8,128)S(1)}, f32[1,16,32,128]{3,2,1,0:T(8,128)S(1)}, u32[]{:S(2)}, u32[]{:S(2)}) collective-permute-start(f32[1,16,32,128]{3,2,1,0:T(8,128)S(1)} %collective-permute-done.2), channel_id=1, source_target_pairs={{0,64},{8,72},{16,80},{24,88},{32,96},{40,104},{48,112},{56,120},{... | collective-permute-start | bytes 786440 | tf_op jit(solution)/shard_map/ppermute | solution.py:13
  203.5 24.7 %collective-permute-start.6 = (f32[1,32,128]{2,1,0:T(8,128)S(1)}, f32[1,32,128]{2,1,0:T(8,128)S(1)}, u32[]{:S(2)}, u32[]{:S(2)}) collective-permute-start(f32[1,32,128]{2,1,0:T(8,128)S(1)} %broadcast.112), channel_id=1, source_target_pairs={{0,128},{8,136},{16,144},{24,152},{32,160},{40,168},{48,176},{56,1... | collective-permute-start | bytes 49160 | tf_op jit(solution)/shard_map/ppermute | solution.py:19
  209.6 4.2 collective-permute-start.4
  212.5 459.1 %collective-permute-start.7 = (f32[1,32,128]{2,1,0:T(8,128)S(1)}, f32[1,32,128]{2,1,0:T(8,128)S(1)}, u32[]{:S(2)}, u32[]{:S(2)}) collective-permute-start(f32[1,32,128]{2,1,0:T(8,128)S(1)} %broadcast.112), channel_id=1, source_target_pairs={{128,0},{136,8},{144,16},{152,24},{160,32},{168,40},{176,48},{184,... | collective-permute-start | bytes 49160 | tf_op jit(solution)/shard_map/ppermute | solution.py:19
  213.8 10.7 %collective-permute-start.5 = (f32[1,16,32,128]{3,2,1,0:T(8,128)S(1)}, f32[1,16,32,128]{3,2,1,0:T(8,128)}, u32[]{:S(2)}, u32[]{:S(2)}) collective-permute-start(f32[1,16,32,128]{3,2,1,0:T(8,128)S(1)} %collective-permute-done.4), channel_id=1, source_target_pairs={{0,16},{8,24},{16,0},{24,8},{32,48},{40,56},{48,32},{56,40},{64,80... | collective-permute-start | bytes 786440 | tf_op jit(solution)/shard_map/ppermute | solution.py:13
  672.5 12.3 %collective-permute-start.16 = (f32[16,32,1]{2,1,0:T(8,128)S(1)}, f32[16,32,1]{2,1,0:T(8,128)S(1)}, u32[]{:S(2)}, u32[]{:S(2)}) collective-permute-start(f32[16,32,1]{2,1,0:T(8,128)S(1)} %get-tuple-element.22), channel_id=1, source_target_pairs={{0,8},{8,16},{16,24},{24,32},{32,40},{40,48},{48,56},{56,64},{64,7... | collective-permute-start | bytes 6152 | tf_op jit(solution)/shard_map/ppermute | solution.py:19
  674.2 12.0 %collective-permute-start.17 = (f32[16,32,1]{2,1,0:T(8,128)S(1)}, f32[16,32,1]{2,1,0:T(8,128)S(1)}, u32[]{:S(2)}, u32[]{:S(2)}) collective-permute-start(f32[16,32,1]{2,1,0:T(8,128)S(1)} %get-tuple-element.23), channel_id=1, source_target_pairs={{8,0},{16,8},{24,16},{32,24},{40,32},{48,40},{56,48},{64,56},{72,6... | collective-permute-start | bytes 6152 | tf_op jit(solution)/shard_map/ppermute | solution.py:19
  675.5 10.7 %collective-permute-start.15 = (f32[16,1,128]{2,1,0:T(1,128)S(1)}, f32[16,1,128]{2,1,0:T(1,128)S(1)}, u32[]{:S(2)}, u32[]{:S(2)}) collective-permute-start(f32[16,1,128]{2,1,0:T(1,128)S(1)} %get-tuple-element.21), channel_id=1, source_target_pairs={{32,0},{40,8},{48,16},{56,24},{64,32},{72,40},{80,48},{88,56},{96,... | collective-permute-start | bytes 24584 | tf_op jit(solution)/shard_map/ppermute | solution.py:19
  676.8 9.4 %collective-permute-start.14 = (f32[16,1,128]{2,1,0:T(1,128)S(1)}, f32[16,1,128]{2,1,0:T(1,128)S(1)}, u32[]{:S(2)}, u32[]{:S(2)}) collective-permute-start(f32[16,1,128]{2,1,0:T(1,128)S(1)} %get-tuple-element.20), channel_id=1, source_target_pairs={{0,32},{8,40},{16,48},{24,56},{32,64},{40,72},{48,80},{56,88},{64,... | collective-permute-start | bytes 24584 | tf_op jit(solution)/shard_map/ppermute | solution.py:19
  682.2 4.0 collective-permute-start.12
  684.8 5.6 collective-permute-start.13
  690.9 21.5 %collective-permute-start.22 = (f32[16,32,1]{2,1,0:T(8,128)S(1)}, f32[16,32,1]{2,1,0:T(8,128)S(1)}, u32[]{:S(2)}, u32[]{:S(2)}) collective-permute-start(f32[16,32,1]{2,1,0:T(8,128)S(1)} %get-tuple-element.16), channel_id=1, source_target_pairs={{0,8},{8,16},{16,24},{24,32},{32,40},{40,48},{48,56},{56,64},{64,7... | collective-permute-start | bytes 6152 | tf_op jit(solution)/shard_map/ppermute | solution.py:19
  692.2 21.5 %collective-permute-start.23 = (f32[16,32,1]{2,1,0:T(8,128)S(1)}, f32[16,32,1]{2,1,0:T(8,128)S(1)}, u32[]{:S(2)}, u32[]{:S(2)}) collective-permute-start(f32[16,32,1]{2,1,0:T(8,128)S(1)} %get-tuple-element.17), channel_id=1, source_target_pairs={{8,0},{16,8},{24,16},{32,24},{40,32},{48,40},{56,48},{64,56},{72,6... | collective-permute-start | bytes 6152 | tf_op jit(solution)/shard_map/ppermute | solution.py:19
  693.5 20.2 %collective-permute-start.21 = (f32[16,1,128]{2,1,0:T(1,128)S(1)}, f32[16,1,128]{2,1,0:T(1,128)S(1)}, u32[]{:S(2)}, u32[]{:S(2)}) collective-permute-start(f32[16,1,128]{2,1,0:T(1,128)S(1)} %get-tuple-element.15), channel_id=1, source_target_pairs={{32,0},{40,8},{48,16},{56,24},{64,32},{72,40},{80,48},{88,56},{96,... | collective-permute-start | bytes 24584 | tf_op jit(solution)/shard_map/ppermute | solution.py:19
  694.8 18.9 %collective-permute-start.20 = (f32[16,1,128]{2,1,0:T(1,128)S(1)}, f32[16,1,128]{2,1,0:T(1,128)S(1)}, u32[]{:S(2)}, u32[]{:S(2)}) collective-permute-start(f32[16,1,128]{2,1,0:T(1,128)S(1)} %get-tuple-element.14), channel_id=1, source_target_pairs={{0,32},{8,40},{16,48},{24,56},{32,64},{40,72},{48,80},{56,88},{64,... | collective-permute-start | bytes 24584 | tf_op jit(solution)/shard_map/ppermute | solution.py:19
  700.4 13.4 %collective-permute-start.18 = (f32[1,32,128]{2,1,0:T(8,128)S(1)}, f32[1,32,128]{2,1,0:T(8,128)S(1)}, u32[]{:S(2)}, u32[]{:S(2)}) collective-permute-start(f32[1,32,128]{2,1,0:T(8,128)S(1)} %get-tuple-element.12), channel_id=1, source_target_pairs={{0,128},{8,136},{16,144},{24,152},{32,160},{40,168},{48,176},{56,1... | collective-permute-start | bytes 49160 | tf_op jit(solution)/shard_map/ppermute | solution.py:19
  712.4 5.6 collective-permute-start.19
  718.5 21.8 %collective-permute-start.28 = (f32[16,32,1]{2,1,0:T(8,128)S(1)}, f32[16,32,1]{2,1,0:T(8,128)S(1)}, u32[]{:S(2)}, u32[]{:S(2)}) collective-permute-start(f32[16,32,1]{2,1,0:T(8,128)S(1)} %get-tuple-element.10), channel_id=1, source_target_pairs={{0,8},{8,16},{16,24},{24,32},{32,40},{40,48},{48,56},{56,64},{64,7... | collective-permute-start | bytes 6152 | tf_op jit(solution)/shard_map/ppermute | solution.py:19
  719.8 21.8 %collective-permute-start.29 = (f32[16,32,1]{2,1,0:T(8,128)S(1)}, f32[16,32,1]{2,1,0:T(8,128)S(1)}, u32[]{:S(2)}, u32[]{:S(2)}) collective-permute-start(f32[16,32,1]{2,1,0:T(8,128)S(1)} %get-tuple-element.11), channel_id=1, source_target_pairs={{8,0},{16,8},{24,16},{32,24},{40,32},{48,40},{56,48},{64,56},{72,6... | collective-permute-start | bytes 6152 | tf_op jit(solution)/shard_map/ppermute | solution.py:19
  721.1 20.5 %collective-permute-start.27 = (f32[16,1,128]{2,1,0:T(1,128)S(1)}, f32[16,1,128]{2,1,0:T(1,128)S(1)}, u32[]{:S(2)}, u32[]{:S(2)}) collective-permute-start(f32[16,1,128]{2,1,0:T(1,128)S(1)} %get-tuple-element.9), channel_id=1, source_target_pairs={{32,0},{40,8},{48,16},{56,24},{64,32},{72,40},{80,48},{88,56},{96,... | collective-permute-start | bytes 24584 | tf_op jit(solution)/shard_map/ppermute | solution.py:19
  722.4 19.3 %collective-permute-start.26 = (f32[16,1,128]{2,1,0:T(1,128)S(1)}, f32[16,1,128]{2,1,0:T(1,128)S(1)}, u32[]{:S(2)}, u32[]{:S(2)}) collective-permute-start(f32[16,1,128]{2,1,0:T(1,128)S(1)} %get-tuple-element.8), channel_id=1, source_target_pairs={{0,32},{8,40},{16,48},{24,56},{32,64},{40,72},{48,80},{56,88},{64,... | collective-permute-start | bytes 24584 | tf_op jit(solution)/shard_map/ppermute | solution.py:19
  727.9 13.8 %collective-permute-start.24 = (f32[1,32,128]{2,1,0:T(8,128)S(1)}, f32[1,32,128]{2,1,0:T(8,128)S(1)}, u32[]{:S(2)}, u32[]{:S(2)}) collective-permute-start(f32[1,32,128]{2,1,0:T(8,128)S(1)} %get-tuple-element.6), channel_id=1, source_target_pairs={{0,128},{8,136},{16,144},{24,152},{32,160},{40,168},{48,176},{56,1... | collective-permute-start | bytes 49160 | tf_op jit(solution)/shard_map/ppermute | solution.py:19
  740.3 5.6 collective-permute-start.25
  (3 other events, 554.9 us)
Sparse Core Ops, SparseCore 0:
  11.8 121.2 all-gather.2
